TPU v7x, 256 devices: a whole 4x4x8 slice. The times are simulated.
256 devices in a mesh: lon: 32 (over x, z_lo, core), lat: 8 (over y, z_hi).
Axes of the slice: x: 4, y: 4, z: 8 (z_hi: 2, z_lo: 4; z = z_hi * 4 + z_lo), core: 2. Of those that a mesh axis runs over, the one named last changes fastest.
Arguments:
- state: float32 [3, 256, 64, 8192], P(None, None, 'lat', 'lon'), may hold values from -6 to 6
- bathymetry: float32 [64, 8192], P('lat', 'lon'), may hold values from 0.5 to 2
- obs_index: int32 [8, 32, 256], P('lat', 'lon'), may hold values from 0 to 2047
- obs_count: int32 [8, 32], P('lat', 'lon'), may hold values from 85 to 256, as said below
- obs_value: float32 [8, 32, 256], P('lat', 'lon'), may hold values from -6 to 6
- obs_sd: float32 [8, 32, 256], P('lat', 'lon'), may hold values from 0.5 to 2
Outputs:
- analysis: float32 [3, 256, 64, 8192], P(None, None, 'lat', 'lon')
Inputs may be any that keep to these rules, and one draw needn't show every extreme that they name: `obs_count`: at least 85 slots of every tile are used; at least one tile uses all 256. `obs_index`: several slots may name the same cell.
All inputs are finite; a program needn't handle non-finite values.
Results may differ from a plain program's by a relative error of at most 0.000051.
Values sent between devices are 32-bit elements; how exact they have to be, the bound alone decides.
No kernel may reach another device: no remote copies, remote signals or barrier semaphores. Data moves between devices by JAX's collectives and lax.ppermute only.
A program may use at most 128 MiB of HBM per device.

v0:
```python
import math
import jax
import jax.numpy as jnp
from jax import lax
from jax.sharding import PartitionSpec as P


def with_halo(value, sides, width, wrap):
    for axis, dim in sides:
        count, length = (lax.axis_size(axis), value.shape[dim])
        up = [(i, (i + 1) % count) for i in range(count if wrap else count - 1)]
        down = [(j, i) for i, j in up]
        last = lax.slice_in_dim(value, length - width, length, axis=dim)
        first = lax.slice_in_dim(value, 0, width, axis=dim)
        before = lax.ppermute(last, axis, up)
        after = lax.ppermute(first, axis, down)
        value = jnp.concatenate([before, value, after], axis=dim)
    return value


def coriolis(rows, total):
    return jnp.sin(math.pi / 3.0 * ((rows.astype(jnp.float32) + 0.5) / total - 0.5))[:, None]


def extend(field, width):
    wide = with_halo(field, (("lat", 2),), width, False)
    return with_halo(wide, (("lon", 3),), width, True)


def new_height(height, flux, keep):
    div = (
        flux[0][:, 1:-1, 2:] - flux[0][:, 1:-1, :-2] + flux[1][:, 2:, 1:-1] - flux[1][:, :-2, 1:-1]
    )
    return (height - 0.25 * div) * keep


def new_wind(east, north, height, fcor, keep):
    grad_x = height[:, 1:-1, 2:] - height[:, 1:-1, :-2]
    grad_y = height[:, 2:, 1:-1] - height[:, :-2, 1:-1]
    east_new = (east + 0.5 * (fcor * north - 0.5 * grad_x)) * keep
    north_new = (north - 0.5 * (fcor * east + 0.5 * grad_y)) * keep
    return (east_new, north_new)


def shards(state, bathymetry, obs_index, obs_count, obs_value, obs_sd):
    members, nrows, ncols = (state.shape[1], state.shape[2], state.shape[3])
    total_rows = nrows * lax.axis_size("lat")
    base = lax.axis_index("lat") * nrows
    fcor = coriolis(base + jnp.arange(nrows), total_rows)
    height, east, north = (state[0], state[1], state[2])
    for step in range(2):
        flux = extend(jnp.stack([bathymetry * east, bathymetry * north]), 1)
        height = new_height(height, flux, 1.0)
        tall = extend(height[None], 1)[0]
        east, north = new_wind(east, north, tall, fcor, 1.0)
    slots = obs_index.shape[2]
    flat_height = height.reshape(members, nrows * ncols)
    hx = jnp.take(flat_height, obs_index.reshape(-1), axis=1)
    valid = (jnp.arange(slots) < obs_count.reshape(())).astype(jnp.float32)
    sigma = obs_sd.reshape(-1) * (
        math.sqrt(slots * lax.axis_size("lat") * lax.axis_size("lon")) / 16.0
    )
    hmean = jnp.mean(hx, axis=0)
    anomal = (hx - hmean) / (math.sqrt(members - 1) * sigma) * valid
    innov = (obs_value.reshape(-1) - hmean) / sigma * valid
    gram = jnp.dot(anomal, anomal.T, precision=lax.Precision.HIGHEST)
    proj = jnp.dot(anomal, innov, precision=lax.Precision.HIGHEST)
    gram, proj = lax.psum((gram, proj), ("lon", "lat"))
    eye = jnp.eye(members, dtype=jnp.float32)
    lower = jnp.linalg.cholesky(gram + eye)
    inv_lower = jax.scipy.linalg.solve_triangular(lower, eye, lower=True)
    weights = jax.scipy.linalg.cho_solve((lower, True), proj)
    transform = inv_lower.T + weights[:, None] / math.sqrt(members - 1)
    fields = jnp.stack([height, east, north])
    center = jnp.mean(fields, axis=1, keepdims=True)
    mixed = jnp.einsum("nm,cnab->cmab", transform, fields - center, precision=lax.Precision.HIGHEST)
    return center + mixed


def solution(mesh):
    return jax.shard_map(
        shards,
        mesh=mesh,
        in_specs=(
            P(None, None, "lat", "lon"),
            P("lat", "lon"),
            P("lat", "lon", None),
            P("lat", "lon"),
            P("lat", "lon", None),
            P("lat", "lon", None),
        ),
        out_specs=P(None, None, "lat", "lon"),
        check_vma=False,
    )
```

profile of v0, /device:TPU:8, one launch (start us, length us, event | category | flops | bytes accessed | tf_op | source)
XLA Modules:
  0.0 587.8 jit_solution(7116847816058828899)
XLA Ops:
  27.2 9.1 %collective-permute-start = (f32[2,256,1,256]{1,0,3,2:T(2,128)S(1)}, f32[2,256,1,256]{1,0,3,2:T(2,128)S(1)}, u32[]{:S(2)}, u32[]{:S(2)}) collective-permute-start(f32[2,256,1,256]{1,0,3,2:T(2,128)S(1)} %get-tuple-element.44), channel_id=1, source_target_pairs={{0,1},{1,2},{2,3},{3,4},{4,5},{5,6},{6,7},{8,9},{9,10},{10,11},{11... | collective-permute-start | bytes 1572872 | tf_op jit(solution)/shard_map/ppermute | solution.py:15
  38.3 12.9 %collective-permute-done = f32[2,256,1,256]{1,0,3,2:T(2,128)S(1)} collective-permute-done((f32[2,256,1,256]{1,0,3,2:T(2,128)S(1)}, f32[2,256,1,256]{1,0,3,2:T(2,128)S(1)}, u32[]{:S(2)}, u32[]{:S(2)}) %collective-permute-start) | collective-permute-done | bytes 524320 | tf_op jit(solution)/shard_map/ppermute | solution.py:15
  51.2 30.3 %collective-permute-done.1 = f32[2,256,1,256]{1,0,3,2:T(2,128)S(1)} collective-permute-done((f32[2,256,1,256]{1,0,3,2:T(2,128)S(1)}, f32[2,256,1,256]{1,0,3,2:T(2,128)S(1)}, u32[]{:S(2)}, u32[]{:S(2)}) %collective-permute-start.1) | collective-permute-done | bytes 524320 | tf_op jit(solution)/shard_map/ppermute | solution.py:16
  81.6 5.9 %collective-permute-start.3 = (f32[2,256,10,1]{1,0,3,2:T(2,128)S(1)}, f32[2,256,10,1]{1,0,3,2:T(2,128)S(1)}, u32[]{:S(2)}, u32[]{:S(2)}) collective-permute-start(f32[2,256,10,1]{1,0,3,2:T(2,128)S(1)} %get-tuple-element.41), channel_id=1, source_target_pairs={{8,0},{16,8},{24,16},{32,24},{40,32},{48,40},{56,48},{64,56},{72,6... | collective-permute-start | bytes 61448 | tf_op jit(solution)/shard_map/ppermute | solution.py:16
  90.4 9.7 %pad_maximum_fusion.2 = f32[2,256,10,258]{1,0,3,2:T(2,128)} fusion(f32[2,256,10,1]{1,0,3,2:T(2,128)S(1)} %collective-permute-done.3, f32[2,256,1,256]{1,0,3,2:T(2,128)S(1)} %collective-permute-done.1, f32[1,256,8,256]{1,0,3,2:T(1,128)} %copy-done, f32[1,256,8,256]{1,0,3,2:T(1,128)S(1)} %copy.43, f32[2,256,1,256]{1,0,3,2:T(2,128)S(1)} %collective-permute-done, ...), kind=kLoop, calls=%fused_computation.8 | loop fusion | flops 6604800 | bytes 10567680 | tf_op jit(solution)/shard_map/concatenate | solution.py:17
  100.1 10.4 %fusion.63 = (f32[1,256,10,258]{1,0,3,2:T(1,128)S(1)}, f32[1,256,10,258]{1,0,3,2:T(1,128)}) fusion(f32[2,256,10,258]{1,0,3,2:T(2,128)} %pad_maximum_fusion.2), kind=kLoop, calls=%fused_computation.141 | loop fusion | bytes 10567680 | tf_op jit(solution)/shard_map/slice | solution.py:32
  113.6 9.3 %collective-permute-start.4 = (f32[1,256,1,256]{1,3,2,0:T(8,128)S(1)}, f32[1,256,1,256]{1,3,2,0:T(8,128)S(1)}, u32[]{:S(2)}, u32[]{:S(2)}) collective-permute-start(f32[1,256,1,256]{1,3,2,0:T(8,128)S(1)} %get-tuple-element.52), channel_id=1, source_target_pairs={{0,1},{1,2},{2,3},{3,4},{4,5},{5,6},{6,7},{8,9},{9,10},{10,11},{11... | collective-permute-start | bytes 786440 | tf_op jit(solution)/shard_map/ppermute | solution.py:15
  125.0 10.7 %collective-permute-done.4 = f32[1,256,1,256]{1,3,2,0:T(8,128)S(1)} collective-permute-done((f32[1,256,1,256]{1,3,2,0:T(8,128)S(1)}, f32[1,256,1,256]{1,3,2,0:T(8,128)S(1)}, u32[]{:S(2)}, u32[]{:S(2)}) %collective-permute-start.4) | collective-permute-done | bytes 262176 | tf_op jit(solution)/shard_map/ppermute | solution.py:15
  135.7 6.7 %collective-permute-done.5 = f32[1,256,1,256]{1,3,2,0:T(8,128)S(1)} collective-permute-done((f32[1,256,1,256]{1,3,2,0:T(8,128)S(1)}, f32[1,256,1,256]{1,3,2,0:T(8,128)S(1)}, u32[]{:S(2)}, u32[]{:S(2)}) %collective-permute-start.5) | collective-permute-done | bytes 262176 | tf_op jit(solution)/shard_map/ppermute | solution.py:16
  144.1 5.8 collective-permute-start.7
  164.1 6.4 %collective-permute-start.8 = (f32[2,256,1,256]{1,3,2,0:T(8,128)S(1)}, f32[2,256,1,256]{1,3,2,0:T(8,128)S(1)}, u32[]{:S(2)}, u32[]{:S(2)}) collective-permute-start(f32[2,256,1,256]{1,3,2,0:T(8,128)S(1)} %get-tuple-element.42), channel_id=1, source_target_pairs={{0,1},{1,2},{2,3},{3,4},{4,5},{5,6},{6,7},{8,9},{9,10},{10,11},{11... | collective-permute-start | bytes 1572872 | tf_op jit(solution)/shard_map/ppermute | solution.py:15
  176.5 17.5 %collective-permute-done.8 = f32[2,256,1,256]{1,3,2,0:T(8,128)S(1)} collective-permute-done((f32[2,256,1,256]{1,3,2,0:T(8,128)S(1)}, f32[2,256,1,256]{1,3,2,0:T(8,128)S(1)}, u32[]{:S(2)}, u32[]{:S(2)}) %collective-permute-start.8) | collective-permute-done | bytes 524320 | tf_op jit(solution)/shard_map/ppermute | solution.py:15
  194.2 7.5 %collective-permute-start.11 = (f32[2,256,10,1]{1,0,3,2:T(2,128)S(1)}, f32[2,256,10,1]{1,0,3,2:T(2,128)S(1)}, u32[]{:S(2)}, u32[]{:S(2)}) collective-permute-start(f32[2,256,10,1]{1,0,3,2:T(2,128)S(1)} %copy.50), channel_id=1, source_target_pairs={{8,0},{16,8},{24,16},{32,24},{40,32},{48,40},{56,48},{64,56},{72,6... | collective-permute-start | bytes 61448 | tf_op jit(solution)/shard_map/ppermute | solution.py:16
  202.1 13.5 %collective-permute-done.10 = f32[2,256,10,1]{1,0,3,2:T(2,128)S(1)} collective-permute-done((f32[2,256,10,1]{1,0,3,2:T(2,128)S(1)}, f32[2,256,10,1]{1,0,3,2:T(2,128)S(1)}, u32[]{:S(2)}, u32[]{:S(2)}) %collective-permute-start.10) | collective-permute-done | bytes 20512 | tf_op jit(solution)/shard_map/ppermute | solution.py:15
  223.9 7.3 %collective-permute-start.12 = (f32[1,256,1,256]{1,3,2,0:T(8,128)}, f32[1,256,1,256]{1,3,2,0:T(8,128)S(1)}, u32[]{:S(2)}, u32[]{:S(2)}) collective-permute-start(f32[1,256,1,256]{1,3,2,0:T(8,128)} %get-tuple-element.50), channel_id=1, source_target_pairs={{0,1},{1,2},{2,3},{3,4},{4,5},{5,6},{6,7},{8,9},{9,10},{10,11},{11... | collective-permute-start | bytes 786440 | tf_op jit(solution)/shard_map/ppermute | solution.py:15
  231.2 5.8 collective-permute-start.13
  237.2 79.0 %psum.15 = f32[256]{0:T(256)S(1)} all-reduce(f32[256]{0:T(256)S(1)} %bitcast.156), channel_id=1, replica_groups=mesh['lon'=32,'lat'=8] {'lon','lat'}, use_global_device_ids=true, to_apply=%region_7.8 | all-reduce | flops 256 | bytes 2048 | tf_op jit(solution)/shard_map/psum | solution.py:68
  316.2 167.4 %all-reduce.3.cloned.1.call-done = f32[256,256]{0,1:T(8,128)} async-done(((f32[256,256]{0,1:T(8,128)}), f32[256,256]{0,1:T(8,128)}) %all-reduce.3.cloned.1.call-update) | async-done | bytes 262160 | tf_op jit(solution)/shard_map/psum | solution.py:68
  485.8 11.7 %cholesky.49 = f32[128,128]{1,0:T(8,128)S(1)} custom-call(f32[128,128]{1,0:T(8,128)S(1)} %cholesky.115), custom_call_target="Cholesky" | custom-call | tf_op jit(solution)/shard_map/jit(cholesky)/cholesky | solution.py:70
  497.5 9.8 %custom-call.21 = f32[1,128,128]{1,2,0:T(8,128)S(1)} custom-call(f32[1,128,128]{2,1,0:T(8,128)S(1)} %get-tuple-element.57), custom_call_target="InvertDiagBlocksLowerTriangular" | custom-call | tf_op jit(solution)/shard_map/jit(cholesky)/cholesky | solution.py:70
  507.8 11.7 %cholesky.103 = f32[128,128]{1,0:T(8,128)S(1)} custom-call(f32[128,128]{1,0:T(8,128)S(1)} %convolution_subtract_fusion.1), custom_call_target="Cholesky" | custom-call | tf_op jit(solution)/shard_map/jit(cholesky)/cholesky | solution.py:70
  527.5 20.6 %custom-call.22 = f32[2,128,128]{1,2,0:T(8,128)S(1)} custom-call(f32[2,128,128]{2,1,0:T(8,128)} %get-tuple-element.12), custom_call_target="InvertDiagBlocksLowerTriangular" | custom-call | tf_op jit(solution)/shard_map/jit(_solve_triangular)/triangular_solve | solution.py:71
  567.0 7.1 %add_bitcast_fusion = f32[3,256,8,256]{1,3,2,0:T(8,128)} fusion(f32[3,8,256]{2,1,0:T(8,128)S(1)} %broadcast_multiply_fusion.2, f32[1,256,8,256]{1,3,2,0:T(8,128)S(1)} %get-tuple-element.30, f32[1,256,8,256]{1,3,2,0:T(8,128)S(1)} %get-tuple-element.29, f32[1,256,8,256]{1,3,2,0:T(8,128)S(1)} %bitcast.145, f32[128,256]{1,0:T(8,128)S(1)} %fusion.48, ...), kind=kOutput, calls=%fused_computation.4 | convolution fusion | flops 4838260736 | bytes 12870656 | tf_op jit(solution)/shard_map/nm,cnab->cmab/dot_general | solution.py:76
  574.0 6.6 %copy.59 = f32[3,256,8,256]{3,2,1,0:T(8,128)} copy(f32[3,256,8,256]{1,3,2,0:T(8,128)} %add_bitcast_fusion) | data formatting | bytes 12582912 | tf_op jit(solution)/shard_map/add | solution.py:77
  (148 shorter events, 93.8 us)
Async XLA Ops:
  6.5 477.1 %all-reduce.3.cloned.1.call-start = ((), (), s32[]{:S(2)}) async-start(), calls=%async_computation | async-start | bytes 524288 | tf_op jit(solution)/shard_map/psum | solution.py:68
  26.3 55.2 %copy-start = (f32[1,256,8,256]{1,0,3,2:T(1,128)}, f32[1,256,8,256]{1,0,3,2:T(1,128)S(1)}, u32[]{:S(2)}) copy-start(f32[1,256,8,256]{1,0,3,2:T(1,128)S(1)} %broadcast_multiply_fusion) | copy-start | bytes 6291460
  27.2 24.0 %collective-permute-start = (f32[2,256,1,256]{1,0,3,2:T(2,128)S(1)}, f32[2,256,1,256]{1,0,3,2:T(2,128)S(1)}, u32[]{:S(2)}, u32[]{:S(2)}) collective-permute-start(f32[2,256,1,256]{1,0,3,2:T(2,128)S(1)} %get-tuple-element.44), channel_id=1, source_target_pairs={{0,1},{1,2},{2,3},{3,4},{4,5},{5,6},{6,7},{8,9},{9,10},{10,11},{11... | collective-permute-start | bytes 1572872 | tf_op jit(solution)/shard_map/ppermute | solution.py:15
  36.3 45.1 %collective-permute-start.1 = (f32[2,256,1,256]{1,0,3,2:T(2,128)S(1)}, f32[2,256,1,256]{1,0,3,2:T(2,128)S(1)}, u32[]{:S(2)}, u32[]{:S(2)}) collective-permute-start(f32[2,256,1,256]{1,0,3,2:T(2,128)S(1)} %get-tuple-element.45), channel_id=1, source_target_pairs={{1,0},{2,1},{3,2},{4,3},{5,4},{6,5},{7,6},{9,8},{10,9},{11,10},{12... | collective-permute-start | bytes 1572872 | tf_op jit(solution)/shard_map/ppermute | solution.py:16
  81.5 8.9 %collective-permute-start.2 = (f32[2,256,10,1]{1,0,3,2:T(2,128)S(1)}, f32[2,256,10,1]{1,0,3,2:T(2,128)S(1)}, u32[]{:S(2)}, u32[]{:S(2)}) collective-permute-start(f32[2,256,10,1]{1,0,3,2:T(2,128)S(1)} %get-tuple-element.40), channel_id=1, source_target_pairs={{0,8},{8,16},{16,24},{24,32},{32,40},{40,48},{48,56},{56,64},{64,7... | collective-permute-start | bytes 61448 | tf_op jit(solution)/shard_map/ppermute | solution.py:15
  81.6 8.8 %collective-permute-start.3 = (f32[2,256,10,1]{1,0,3,2:T(2,128)S(1)}, f32[2,256,10,1]{1,0,3,2:T(2,128)S(1)}, u32[]{:S(2)}, u32[]{:S(2)}) collective-permute-start(f32[2,256,10,1]{1,0,3,2:T(2,128)S(1)} %get-tuple-element.41), channel_id=1, source_target_pairs={{8,0},{16,8},{24,16},{32,24},{40,32},{48,40},{56,48},{64,56},{72,6... | collective-permute-start | bytes 61448 | tf_op jit(solution)/shard_map/ppermute | solution.py:16
  112.9 12.0 %copy-start.16 = (s32[1,1,256]{2,1,0:T(1,128)S(1)}, s32[1,1,256]{2,1,0:T(1,128)}, u32[]{:S(2)}) copy-start(s32[1,1,256]{2,1,0:T(1,128)} %param.8) | copy-start | bytes 3076
  113.6 29.0 %copy-start.2 = (f32[256,8,256]{0,2,1:T(8,128)}, f32[256,8,256]{0,2,1:T(8,128)S(1)}, u32[]{:S(2)}) copy-start(f32[256,8,256]{0,2,1:T(8,128)S(1)} %fusion.27) | copy-start | bytes 6291460
  113.6 22.0 %collective-permute-start.4 = (f32[1,256,1,256]{1,3,2,0:T(8,128)S(1)}, f32[1,256,1,256]{1,3,2,0:T(8,128)S(1)}, u32[]{:S(2)}, u32[]{:S(2)}) collective-permute-start(f32[1,256,1,256]{1,3,2,0:T(8,128)S(1)} %get-tuple-element.52), channel_id=1, source_target_pairs={{0,1},{1,2},{2,3},{3,4},{4,5},{5,6},{6,7},{8,9},{9,10},{10,11},{11... | collective-permute-start | bytes 786440 | tf_op jit(solution)/shard_map/ppermute | solution.py:15
  123.0 19.3 %collective-permute-start.5 = (f32[1,256,1,256]{1,3,2,0:T(8,128)S(1)}, f32[1,256,1,256]{1,3,2,0:T(8,128)S(1)}, u32[]{:S(2)}, u32[]{:S(2)}) collective-permute-start(f32[1,256,1,256]{1,3,2,0:T(8,128)S(1)} %get-tuple-element.53), channel_id=1, source_target_pairs={{1,0},{2,1},{3,2},{4,3},{5,4},{6,5},{7,6},{9,8},{10,9},{11,10},{12... | collective-permute-start | bytes 786440 | tf_op jit(solution)/shard_map/ppermute | solution.py:16
  144.1 12.4 %collective-permute-start.6 = (f32[1,256,10,1]{1,3,2,0:T(1,128)S(1)}, f32[1,256,10,1]{1,3,2,0:T(1,128)S(1)}, u32[]{:S(2)}, u32[]{:S(2)}) collective-permute-start(f32[1,256,10,1]{1,3,2,0:T(1,128)S(1)} %get-tuple-element.48), channel_id=1, source_target_pairs={{0,8},{8,16},{16,24},{24,32},{32,40},{40,48},{48,56},{56,64},{64,7... | collective-permute-start | bytes 30728 | tf_op jit(solution)/shard_map/ppermute | solution.py:15
  144.1 12.5 %collective-permute-start.7 = (f32[1,256,10,1]{1,3,2,0:T(1,128)S(1)}, f32[1,256,10,1]{1,3,2,0:T(1,128)S(1)}, u32[]{:S(2)}, u32[]{:S(2)}) collective-permute-start(f32[1,256,10,1]{1,3,2,0:T(1,128)S(1)} %get-tuple-element.49), channel_id=1, source_target_pairs={{8,0},{16,8},{24,16},{32,24},{40,32},{48,40},{56,48},{64,56},{72,6... | collective-permute-start | bytes 30728 | tf_op jit(solution)/shard_map/ppermute | solution.py:16
  150.0 9.3 %copy-start.18 = (f32[8]{0:T(128)}, f32[8]{0:T(128)S(1)}, u32[]{:S(2)}) copy-start(f32[8]{0:T(128)S(1)} %multiply_sine_fusion) | copy-start | bytes 100
  164.0 30.0 %copy-start.1 = (f32[1,256,8,256]{1,3,2,0:T(8,128)}, f32[1,256,8,256]{1,3,2,0:T(8,128)S(1)}, u32[]{:S(2)}) copy-start(f32[1,256,8,256]{1,3,2,0:T(8,128)S(1)} %get-tuple-element.27) | copy-start | bytes 6291460
  164.0 11.9 %copy-start.20 = (f32[1,1,256]{2,1,0:T(1,128)S(1)}, f32[1,1,256]{2,1,0:T(1,128)}, u32[]{:S(2)}) copy-start(f32[1,1,256]{2,1,0:T(1,128)} %param.11) | copy-start | bytes 3076
  164.1 29.9 %collective-permute-start.8 = (f32[2,256,1,256]{1,3,2,0:T(8,128)S(1)}, f32[2,256,1,256]{1,3,2,0:T(8,128)S(1)}, u32[]{:S(2)}, u32[]{:S(2)}) collective-permute-start(f32[2,256,1,256]{1,3,2,0:T(8,128)S(1)} %get-tuple-element.42), channel_id=1, source_target_pairs={{0,1},{1,2},{2,3},{3,4},{4,5},{5,6},{6,7},{8,9},{9,10},{10,11},{11... | collective-permute-start | bytes 1572872 | tf_op jit(solution)/shard_map/ppermute | solution.py:15
  170.5 23.5 %collective-permute-start.9 = (f32[2,256,1,256]{1,3,2,0:T(8,128)S(1)}, f32[2,256,1,256]{1,3,2,0:T(8,128)S(1)}, u32[]{:S(2)}, u32[]{:S(2)}) collective-permute-start(f32[2,256,1,256]{1,3,2,0:T(8,128)S(1)} %get-tuple-element.43), channel_id=1, source_target_pairs={{1,0},{2,1},{3,2},{4,3},{5,4},{6,5},{7,6},{9,8},{10,9},{11,10},{12... | collective-permute-start | bytes 1572872 | tf_op jit(solution)/shard_map/ppermute | solution.py:16
  194.0 21.6 %collective-permute-start.10 = (f32[2,256,10,1]{1,0,3,2:T(2,128)S(1)}, f32[2,256,10,1]{1,0,3,2:T(2,128)S(1)}, u32[]{:S(2)}, u32[]{:S(2)}) collective-permute-start(f32[2,256,10,1]{1,0,3,2:T(2,128)S(1)} %copy.49), channel_id=1, source_target_pairs={{0,8},{8,16},{16,24},{24,32},{32,40},{40,48},{48,56},{56,64},{64,7... | collective-permute-start | bytes 61448 | tf_op jit(solution)/shard_map/ppermute | solution.py:15
  194.2 21.5 %collective-permute-start.11 = (f32[2,256,10,1]{1,0,3,2:T(2,128)S(1)}, f32[2,256,10,1]{1,0,3,2:T(2,128)S(1)}, u32[]{:S(2)}, u32[]{:S(2)}) collective-permute-start(f32[2,256,10,1]{1,0,3,2:T(2,128)S(1)} %copy.50), channel_id=1, source_target_pairs={{8,0},{16,8},{24,16},{32,24},{40,32},{48,40},{56,48},{64,56},{72,6... | collective-permute-start | bytes 61448 | tf_op jit(solution)/shard_map/ppermute | solution.py:16
  223.9 298.5 %copy-start.22 = (s32[2]{0:T(128)S(1)}, s32[2]{0:T(128)}, u32[]{:S(2)}) copy-start(s32[2]{0:T(128)} %iota_multiply_fusion) | copy-start | bytes 28
  223.9 326.5 %collective-permute-start.12 = (f32[1,256,1,256]{1,3,2,0:T(8,128)}, f32[1,256,1,256]{1,3,2,0:T(8,128)S(1)}, u32[]{:S(2)}, u32[]{:S(2)}) collective-permute-start(f32[1,256,1,256]{1,3,2,0:T(8,128)} %get-tuple-element.50), channel_id=1, source_target_pairs={{0,1},{1,2},{2,3},{3,4},{4,5},{5,6},{6,7},{8,9},{9,10},{10,11},{11... | collective-permute-start | bytes 786440 | tf_op jit(solution)/shard_map/ppermute | solution.py:15
  231.2 319.2 %collective-permute-start.13 = (f32[1,256,1,256]{1,3,2,0:T(8,128)}, f32[1,256,1,256]{1,3,2,0:T(8,128)}, u32[]{:S(2)}, u32[]{:S(2)}) collective-permute-start(f32[1,256,1,256]{1,3,2,0:T(8,128)} %get-tuple-element.51), channel_id=1, source_target_pairs={{1,0},{2,1},{3,2},{4,3},{5,4},{6,5},{7,6},{9,8},{10,9},{11,10},{12... | collective-permute-start | bytes 786440 | tf_op jit(solution)/shard_map/ppermute | solution.py:16
  551.6 8.5 %collective-permute-start.14 = (f32[1,256,10,1]{1,3,2,0:T(1,128)S(1)}, f32[1,256,10,1]{1,3,2,0:T(1,128)S(1)}, u32[]{:S(2)}, u32[]{:S(2)}) collective-permute-start(f32[1,256,10,1]{1,3,2,0:T(1,128)S(1)} %get-tuple-element.46), channel_id=1, source_target_pairs={{0,8},{8,16},{16,24},{24,32},{32,40},{40,48},{48,56},{56,64},{64,7... | collective-permute-start | bytes 30728 | tf_op jit(solution)/shard_map/ppermute | solution.py:15
  551.6 8.4 %collective-permute-start.15 = (f32[1,256,10,1]{1,3,2,0:T(1,128)S(1)}, f32[1,256,10,1]{1,3,2,0:T(1,128)S(1)}, u32[]{:S(2)}, u32[]{:S(2)}) collective-permute-start(f32[1,256,10,1]{1,3,2,0:T(1,128)S(1)} %get-tuple-element.47), channel_id=1, source_target_pairs={{8,0},{16,8},{24,16},{32,24},{40,32},{48,40},{56,48},{64,56},{72,6... | collective-permute-start | bytes 30728 | tf_op jit(solution)/shard_map/ppermute | solution.py:16
  (16 other events, 30.3 us)
Sparse Core Ops, SparseCore 0:
  223.2 260.4 all-reduce.2
where the time goes:
time: 594 us; the launch traced here: 588 us
  waiting for transfers between devices  259 us (44%)
  other arithmetic  90 us (15%)
  blocking collectives  79 us (13%)
  starting transfers between devices  71.1 us (12%)
  local copies, waits for them, and re-layouts  61.1 us (10%)
  between operations  16.3 us (3%)
  matrix products  11.2 us (2%)
    psum x1, waiting for transfers between devices, shards(): gram, proj = lax.psum((gram, proj), ('lon', 'lat'))  167 us
    psum x1, blocking collectives, shards(): gram, proj = lax.psum((gram, proj), ('lon', 'lat'))  79 us
    ppermute x8, waiting for transfers between devices, with_halo(): before = lax.ppermute(last, axis, up)  54.6 us
    ppermute x8, starting transfers between devices, with_halo(): after = lax.ppermute(first, axis, down)  38.8 us
    ppermute x8, waiting for transfers between devices, with_halo(): after = lax.ppermute(first, axis, down)  37 us
    another operation x7, other arithmetic, shards(): lower = jnp.linalg.cholesky(gram + eye)  34.7 us
    ppermute x8, starting transfers between devices, with_halo(): before = lax.ppermute(last, axis, up)  32.3 us
    another operation x3, other arithmetic, shards(): inv_lower = jax.scipy.linalg.solve_triangular(lower, eye, lower=True)  21.2 us
  transfers between devices with their start and end apart: 17, of which 7 were waited for; matrix products, arithmetic and copies ran while one was open for 14% of the time, Pallas kernels for 0%

commit v1 on v0

--- a/solution.py
+++ b/solution.py
@@ -65,7 +65,7 @@
     innov = (obs_value.reshape(-1) - hmean) / sigma * valid
     gram = jnp.dot(anomal, anomal.T, precision=lax.Precision.HIGHEST)
     proj = jnp.dot(anomal, innov, precision=lax.Precision.HIGHEST)
-    gram, proj = lax.psum((gram, proj), ("lon", "lat"))
+    gram, proj = lax.psum(lax.psum((gram, proj), "lat"), "lon")
     eye = jnp.eye(members, dtype=jnp.float32)
     lower = jnp.linalg.cholesky(gram + eye)
     inv_lower = jax.scipy.linalg.solve_triangular(lower, eye, lower=True)

time: 594 us -> 728 us (1.23)
  waiting for transfers between devices: 259 us -> 366 us
  blocking collectives: 79 us -> 96.3 us
    psum x1 -> x2, waiting for transfers between devices: 167 us -> 261 us  [shards(): gram, proj = lax.psum(lax.psum((gram, proj), 'lat'), 'lon')]
    psum x1 -> x2, blocking collectives: 79 us -> 96.3 us  [shards(): gram, proj = lax.psum(lax.psum((gram, proj), 'lat'), 'lon')]
    ppermute x8, waiting for transfers between devices: 54.6 us -> 62.9 us  [with_halo(): before = lax.ppermute(last, axis, up)]
    unnamed x52 -> x58, local copies, waits for them, and re-layouts: 20.5 us -> 23.2 us
  transfers between devices with their start and end apart: 17 -> 18, of which waited for: 7 -> 9; matrix products, arithmetic and copies ran while one was open for 14% -> 4% of each run, Pallas kernels for 0% -> 0%
where the time goes in v1:
time: 728 us; the launch traced here: 721 us
  waiting for transfers between devices  366 us (50%)
  blocking collectives  96.3 us (13%)
  other arithmetic  91.4 us (13%)
  starting transfers between devices  71.3 us (10%)
  local copies, waits for them, and re-layouts  66.9 us (9%)
  between operations  16.4 us (2%)
  matrix products  12.7 us (2%)
    psum x2, waiting for transfers between devices, shards(): gram, proj = lax.psum(lax.psum((gram, proj), 'lat'), 'lon')  261 us
    psum x2, blocking collectives, shards(): gram, proj = lax.psum(lax.psum((gram, proj), 'lat'), 'lon')  96.3 us
    ppermute x8, waiting for transfers between devices, with_halo(): before = lax.ppermute(last, axis, up)  62.9 us
    ppermute x8, waiting for transfers between devices, with_halo(): after = lax.ppermute(first, axis, down)  41.4 us
    ppermute x8, starting transfers between devices, with_halo(): after = lax.ppermute(first, axis, down)  39.1 us
    another operation x7, other arithmetic, shards(): lower = jnp.linalg.cholesky(gram + eye)  34.8 us
    ppermute x8, starting transfers between devices, with_halo(): before = lax.ppermute(last, axis, up)  32.1 us
    unnamed x58, local copies, waits for them, and re-layouts  23.2 us
  transfers between devices with their start and end apart: 18, of which 9 were waited for; matrix products, arithmetic and copies ran while one was open for 4% of the time, Pallas kernels for 0%

profile of v1, /device:TPU:8, one launch (start us, length us, event | category | flops | bytes accessed | tf_op | source)
XLA Modules:
  0.0 720.6 jit_solution(6565714652809119836)
XLA Ops:
  27.3 9.1 %collective-permute-start = (f32[2,256,1,256]{1,0,3,2:T(2,128)S(1)}, f32[2,256,1,256]{1,0,3,2:T(2,128)S(1)}, u32[]{:S(2)}, u32[]{:S(2)}) collective-permute-start(f32[2,256,1,256]{1,0,3,2:T(2,128)S(1)} %get-tuple-element.44), channel_id=1, source_target_pairs={{0,1},{1,2},{2,3},{3,4},{4,5},{5,6},{6,7},{8,9},{9,10},{10,11},{11... | collective-permute-start | bytes 1572872 | tf_op jit(solution)/shard_map/ppermute | solution.py:15
  38.4 12.9 %collective-permute-done = f32[2,256,1,256]{1,0,3,2:T(2,128)S(1)} collective-permute-done((f32[2,256,1,256]{1,0,3,2:T(2,128)S(1)}, f32[2,256,1,256]{1,0,3,2:T(2,128)S(1)}, u32[]{:S(2)}, u32[]{:S(2)}) %collective-permute-start) | collective-permute-done | bytes 524320 | tf_op jit(solution)/shard_map/ppermute | solution.py:15
  51.3 30.3 %collective-permute-done.1 = f32[2,256,1,256]{1,0,3,2:T(2,128)S(1)} collective-permute-done((f32[2,256,1,256]{1,0,3,2:T(2,128)S(1)}, f32[2,256,1,256]{1,0,3,2:T(2,128)S(1)}, u32[]{:S(2)}, u32[]{:S(2)}) %collective-permute-start.1) | collective-permute-done | bytes 524320 | tf_op jit(solution)/shard_map/ppermute | solution.py:16
  81.7 6.2 collective-permute-start.3
  90.9 9.7 %pad_maximum_fusion.2 = f32[2,256,10,258]{1,0,3,2:T(2,128)} fusion(f32[2,256,10,1]{1,0,3,2:T(2,128)S(1)} %collective-permute-done.3, f32[2,256,1,256]{1,0,3,2:T(2,128)S(1)} %collective-permute-done.1, f32[1,256,8,256]{1,0,3,2:T(1,128)} %copy-done, f32[1,256,8,256]{1,0,3,2:T(1,128)S(1)} %copy.43, f32[2,256,1,256]{1,0,3,2:T(2,128)S(1)} %collective-permute-done, ...), kind=kLoop, calls=%fused_computation.8 | loop fusion | flops 6604800 | bytes 10567680 | tf_op jit(solution)/shard_map/concatenate | solution.py:17
  100.7 10.3 %fusion.63 = (f32[1,256,10,258]{1,0,3,2:T(1,128)S(1)}, f32[1,256,10,258]{1,0,3,2:T(1,128)}) fusion(f32[2,256,10,258]{1,0,3,2:T(2,128)} %pad_maximum_fusion.2), kind=kLoop, calls=%fused_computation.141 | loop fusion | bytes 10567680 | tf_op jit(solution)/shard_map/slice | solution.py:32
  114.1 9.3 %collective-permute-start.4 = (f32[1,256,1,256]{1,3,2,0:T(8,128)S(1)}, f32[1,256,1,256]{1,3,2,0:T(8,128)S(1)}, u32[]{:S(2)}, u32[]{:S(2)}) collective-permute-start(f32[1,256,1,256]{1,3,2,0:T(8,128)S(1)} %get-tuple-element.52), channel_id=1, source_target_pairs={{0,1},{1,2},{2,3},{3,4},{4,5},{5,6},{6,7},{8,9},{9,10},{10,11},{11... | collective-permute-start | bytes 786440 | tf_op jit(solution)/shard_map/ppermute | solution.py:15
  125.4 10.7 %collective-permute-done.4 = f32[1,256,1,256]{1,3,2,0:T(8,128)S(1)} collective-permute-done((f32[1,256,1,256]{1,3,2,0:T(8,128)S(1)}, f32[1,256,1,256]{1,3,2,0:T(8,128)S(1)}, u32[]{:S(2)}, u32[]{:S(2)}) %collective-permute-start.4) | collective-permute-done | bytes 262176 | tf_op jit(solution)/shard_map/ppermute | solution.py:15
  136.1 6.7 collective-permute-done.5
  164.5 6.3 collective-permute-start.8
  177.0 17.3 %collective-permute-done.8 = f32[2,256,1,256]{1,3,2,0:T(8,128)S(1)} collective-permute-done((f32[2,256,1,256]{1,3,2,0:T(8,128)S(1)}, f32[2,256,1,256]{1,3,2,0:T(8,128)S(1)}, u32[]{:S(2)}, u32[]{:S(2)}) %collective-permute-start.8) | collective-permute-done | bytes 524320 | tf_op jit(solution)/shard_map/ppermute | solution.py:15
  194.5 7.5 %collective-permute-start.11 = (f32[2,256,10,1]{1,0,3,2:T(2,128)S(1)}, f32[2,256,10,1]{1,0,3,2:T(2,128)S(1)}, u32[]{:S(2)}, u32[]{:S(2)}) collective-permute-start(f32[2,256,10,1]{1,0,3,2:T(2,128)S(1)} %copy.50), channel_id=1, source_target_pairs={{8,0},{16,8},{24,16},{32,24},{40,32},{48,40},{56,48},{64,56},{72,6... | collective-permute-start | bytes 61448 | tf_op jit(solution)/shard_map/ppermute | solution.py:16
  202.5 13.5 %collective-permute-done.10 = f32[2,256,10,1]{1,0,3,2:T(2,128)S(1)} collective-permute-done((f32[2,256,10,1]{1,0,3,2:T(2,128)S(1)}, f32[2,256,10,1]{1,0,3,2:T(2,128)S(1)}, u32[]{:S(2)}, u32[]{:S(2)}) %collective-permute-start.10) | collective-permute-done | bytes 20512 | tf_op jit(solution)/shard_map/ppermute | solution.py:15
  221.3 7.2 collective-permute-start.12
  237.2 8.4 %collective-permute-done.12 = f32[1,256,1,256]{1,3,2,0:T(8,128)S(1)} collective-permute-done((f32[1,256,1,256]{1,3,2,0:T(8,128)}, f32[1,256,1,256]{1,3,2,0:T(8,128)S(1)}, u32[]{:S(2)}, u32[]{:S(2)}) %collective-permute-start.12) | collective-permute-done | bytes 262176 | tf_op jit(solution)/shard_map/ppermute | solution.py:15
  257.8 27.8 %psum.30 = f32[256]{0:T(256)S(1)} all-reduce(f32[256]{0:T(256)S(1)} %bitcast.156), channel_id=1, replica_groups=mesh['lon'=32,'lat'=8] {'lat'}, use_global_device_ids=true, to_apply=%region_8.9 | all-reduce | flops 256 | bytes 2048 | tf_op jit(solution)/shard_map/psum | solution.py:68
  285.6 68.6 %psum.31 = f32[256]{0:T(256)S(1)} all-reduce(f32[256]{0:T(256)S(1)} %psum.30), channel_id=1, replica_groups=mesh['lon'=32,'lat'=8] {'lon'}, use_global_device_ids=true, to_apply=%region_9.10 | all-reduce | flops 256 | bytes 2048 | tf_op jit(solution)/shard_map/psum | solution.py:68
  370.3 261.3 %all-reduce.6.cloned.1.call-done = f32[256,256]{0,1:T(8,128)} async-done(((f32[256,256]{0,1:T(8,128)}), f32[256,256]{0,1:T(8,128)}) %all-reduce.6.cloned.1.call-update) | async-done | bytes 262160 | tf_op jit(solution)/shard_map/psum | solution.py:68
  633.7 11.7 %cholesky.49 = f32[128,128]{1,0:T(8,128)S(1)} custom-call(f32[128,128]{1,0:T(8,128)S(1)} %cholesky.115), custom_call_target="Cholesky" | custom-call | tf_op jit(solution)/shard_map/jit(cholesky)/cholesky | solution.py:70
  645.5 9.8 %custom-call.21 = f32[1,128,128]{1,2,0:T(8,128)S(1)} custom-call(f32[1,128,128]{2,1,0:T(8,128)S(1)} %get-tuple-element.57), custom_call_target="InvertDiagBlocksLowerTriangular" | custom-call | tf_op jit(solution)/shard_map/jit(cholesky)/cholesky | solution.py:70
  655.8 11.9 %cholesky.103 = f32[128,128]{1,0:T(8,128)S(1)} custom-call(f32[128,128]{1,0:T(8,128)S(1)} %convolution_subtract_fusion.1), custom_call_target="Cholesky" | custom-call | tf_op jit(solution)/shard_map/jit(cholesky)/cholesky | solution.py:70
  675.5 20.5 %custom-call.22 = f32[2,128,128]{1,2,0:T(8,128)S(1)} custom-call(f32[2,128,128]{2,1,0:T(8,128)} %get-tuple-element.12), custom_call_target="InvertDiagBlocksLowerTriangular" | custom-call | tf_op jit(solution)/shard_map/jit(_solve_triangular)/triangular_solve | solution.py:71
  698.1 8.5 %add_bitcast_fusion = f32[3,256,8,256]{1,3,2,0:T(8,128)} fusion(f32[3,8,256]{2,1,0:T(8,128)S(1)} %broadcast_multiply_fusion.2, f32[1,256,8,256]{1,3,2,0:T(8,128)} %copy-done.5, f32[1,256,8,256]{1,3,2,0:T(8,128)} %copy-done.4, f32[1,256,8,256]{1,3,2,0:T(8,128)S(1)} %bitcast.145, f32[128,256]{1,0:T(8,128)S(1)} %fusion.48, f32[128,256]{1,0:T(8,128)S(1)} %fusion.40, ...), kind=kOutput, calls=%fused_computation.4 | convolution fusion | flops 4838260736 | bytes 12870656 | tf_op jit(solution)/shard_map/nm,cnab->cmab/dot_general | solution.py:76
  706.7 6.6 copy.59
  (158 shorter events, 117.1 us)
Async XLA Ops:
  6.5 353.5 %all-reduce.4.cloned.1.call-start = ((), (), s32[]{:S(2)}) async-start(), calls=%async_computation | async-start | bytes 524288 | tf_op jit(solution)/shard_map/psum | solution.py:68
  26.4 55.2 %copy-start = (f32[1,256,8,256]{1,0,3,2:T(1,128)}, f32[1,256,8,256]{1,0,3,2:T(1,128)S(1)}, u32[]{:S(2)}) copy-start(f32[1,256,8,256]{1,0,3,2:T(1,128)S(1)} %broadcast_multiply_fusion) | copy-start | bytes 6291460
  27.3 24.0 %collective-permute-start = (f32[2,256,1,256]{1,0,3,2:T(2,128)S(1)}, f32[2,256,1,256]{1,0,3,2:T(2,128)S(1)}, u32[]{:S(2)}, u32[]{:S(2)}) collective-permute-start(f32[2,256,1,256]{1,0,3,2:T(2,128)S(1)} %get-tuple-element.44), channel_id=1, source_target_pairs={{0,1},{1,2},{2,3},{3,4},{4,5},{5,6},{6,7},{8,9},{9,10},{10,11},{11... | collective-permute-start | bytes 1572872 | tf_op jit(solution)/shard_map/ppermute | solution.py:15
  36.5 45.1 %collective-permute-start.1 = (f32[2,256,1,256]{1,0,3,2:T(2,128)S(1)}, f32[2,256,1,256]{1,0,3,2:T(2,128)S(1)}, u32[]{:S(2)}, u32[]{:S(2)}) collective-permute-start(f32[2,256,1,256]{1,0,3,2:T(2,128)S(1)} %get-tuple-element.45), channel_id=1, source_target_pairs={{1,0},{2,1},{3,2},{4,3},{5,4},{6,5},{7,6},{9,8},{10,9},{11,10},{12... | collective-permute-start | bytes 1572872 | tf_op jit(solution)/shard_map/ppermute | solution.py:16
  81.6 9.3 %collective-permute-start.2 = (f32[2,256,10,1]{1,0,3,2:T(2,128)S(1)}, f32[2,256,10,1]{1,0,3,2:T(2,128)S(1)}, u32[]{:S(2)}, u32[]{:S(2)}) collective-permute-start(f32[2,256,10,1]{1,0,3,2:T(2,128)S(1)} %get-tuple-element.40), channel_id=1, source_target_pairs={{0,8},{8,16},{16,24},{24,32},{32,40},{40,48},{48,56},{56,64},{64,7... | collective-permute-start | bytes 61448 | tf_op jit(solution)/shard_map/ppermute | solution.py:15
  81.7 9.2 %collective-permute-start.3 = (f32[2,256,10,1]{1,0,3,2:T(2,128)S(1)}, f32[2,256,10,1]{1,0,3,2:T(2,128)S(1)}, u32[]{:S(2)}, u32[]{:S(2)}) collective-permute-start(f32[2,256,10,1]{1,0,3,2:T(2,128)S(1)} %get-tuple-element.41), channel_id=1, source_target_pairs={{8,0},{16,8},{24,16},{32,24},{40,32},{48,40},{56,48},{64,56},{72,6... | collective-permute-start | bytes 61448 | tf_op jit(solution)/shard_map/ppermute | solution.py:16
  114.1 29.0 %copy-start.2 = (f32[256,8,256]{0,2,1:T(8,128)}, f32[256,8,256]{0,2,1:T(8,128)S(1)}, u32[]{:S(2)}) copy-start(f32[256,8,256]{0,2,1:T(8,128)S(1)} %fusion.27) | copy-start | bytes 6291460
  114.1 22.0 %collective-permute-start.4 = (f32[1,256,1,256]{1,3,2,0:T(8,128)S(1)}, f32[1,256,1,256]{1,3,2,0:T(8,128)S(1)}, u32[]{:S(2)}, u32[]{:S(2)}) collective-permute-start(f32[1,256,1,256]{1,3,2,0:T(8,128)S(1)} %get-tuple-element.52), channel_id=1, source_target_pairs={{0,1},{1,2},{2,3},{3,4},{4,5},{5,6},{6,7},{8,9},{9,10},{10,11},{11... | collective-permute-start | bytes 786440 | tf_op jit(solution)/shard_map/ppermute | solution.py:15
  123.4 19.4 %collective-permute-start.5 = (f32[1,256,1,256]{1,3,2,0:T(8,128)S(1)}, f32[1,256,1,256]{1,3,2,0:T(8,128)S(1)}, u32[]{:S(2)}, u32[]{:S(2)}) collective-permute-start(f32[1,256,1,256]{1,3,2,0:T(8,128)S(1)} %get-tuple-element.53), channel_id=1, source_target_pairs={{1,0},{2,1},{3,2},{4,3},{5,4},{6,5},{7,6},{9,8},{10,9},{11,10},{12... | collective-permute-start | bytes 786440 | tf_op jit(solution)/shard_map/ppermute | solution.py:16
  144.6 12.4 %collective-permute-start.6 = (f32[1,256,10,1]{1,3,2,0:T(1,128)S(1)}, f32[1,256,10,1]{1,3,2,0:T(1,128)S(1)}, u32[]{:S(2)}, u32[]{:S(2)}) collective-permute-start(f32[1,256,10,1]{1,3,2,0:T(1,128)S(1)} %get-tuple-element.48), channel_id=1, source_target_pairs={{0,8},{8,16},{16,24},{24,32},{32,40},{40,48},{48,56},{56,64},{64,7... | collective-permute-start | bytes 30728 | tf_op jit(solution)/shard_map/ppermute | solution.py:15
  144.6 12.4 %collective-permute-start.7 = (f32[1,256,10,1]{1,3,2,0:T(1,128)S(1)}, f32[1,256,10,1]{1,3,2,0:T(1,128)S(1)}, u32[]{:S(2)}, u32[]{:S(2)}) collective-permute-start(f32[1,256,10,1]{1,3,2,0:T(1,128)S(1)} %get-tuple-element.49), channel_id=1, source_target_pairs={{8,0},{16,8},{24,16},{32,24},{40,32},{48,40},{56,48},{64,56},{72,6... | collective-permute-start | bytes 30728 | tf_op jit(solution)/shard_map/ppermute | solution.py:16
  164.4 29.9 %copy-start.1 = (f32[1,256,8,256]{1,3,2,0:T(8,128)}, f32[1,256,8,256]{1,3,2,0:T(8,128)S(1)}, u32[]{:S(2)}) copy-start(f32[1,256,8,256]{1,3,2,0:T(8,128)S(1)} %get-tuple-element.27) | copy-start | bytes 6291460
  164.5 29.8 %collective-permute-start.8 = (f32[2,256,1,256]{1,3,2,0:T(8,128)S(1)}, f32[2,256,1,256]{1,3,2,0:T(8,128)S(1)}, u32[]{:S(2)}, u32[]{:S(2)}) collective-permute-start(f32[2,256,1,256]{1,3,2,0:T(8,128)S(1)} %get-tuple-element.42), channel_id=1, source_target_pairs={{0,1},{1,2},{2,3},{3,4},{4,5},{5,6},{6,7},{8,9},{9,10},{10,11},{11... | collective-permute-start | bytes 1572872 | tf_op jit(solution)/shard_map/ppermute | solution.py:15
  170.8 23.5 %collective-permute-start.9 = (f32[2,256,1,256]{1,3,2,0:T(8,128)S(1)}, f32[2,256,1,256]{1,3,2,0:T(8,128)S(1)}, u32[]{:S(2)}, u32[]{:S(2)}) collective-permute-start(f32[2,256,1,256]{1,3,2,0:T(8,128)S(1)} %get-tuple-element.43), channel_id=1, source_target_pairs={{1,0},{2,1},{3,2},{4,3},{5,4},{6,5},{7,6},{9,8},{10,9},{11,10},{12... | collective-permute-start | bytes 1572872 | tf_op jit(solution)/shard_map/ppermute | solution.py:16
  194.4 21.6 %collective-permute-start.10 = (f32[2,256,10,1]{1,0,3,2:T(2,128)S(1)}, f32[2,256,10,1]{1,0,3,2:T(2,128)S(1)}, u32[]{:S(2)}, u32[]{:S(2)}) collective-permute-start(f32[2,256,10,1]{1,0,3,2:T(2,128)S(1)} %copy.49), channel_id=1, source_target_pairs={{0,8},{8,16},{16,24},{24,32},{32,40},{40,48},{48,56},{56,64},{64,7... | collective-permute-start | bytes 61448 | tf_op jit(solution)/shard_map/ppermute | solution.py:15
  194.5 21.5 %collective-permute-start.11 = (f32[2,256,10,1]{1,0,3,2:T(2,128)S(1)}, f32[2,256,10,1]{1,0,3,2:T(2,128)S(1)}, u32[]{:S(2)}, u32[]{:S(2)}) collective-permute-start(f32[2,256,10,1]{1,0,3,2:T(2,128)S(1)} %copy.50), channel_id=1, source_target_pairs={{8,0},{16,8},{24,16},{32,24},{40,32},{48,40},{56,48},{64,56},{72,6... | collective-permute-start | bytes 61448 | tf_op jit(solution)/shard_map/ppermute | solution.py:16
  220.5 15.1 %copy-start.17 = (f32[256]{0:T(256)S(1)}, f32[256]{0:T(256)}, u32[]{:S(2)}) copy-start(f32[256]{0:T(256)} %get-tuple-element.67) | copy-start | bytes 3076
  220.5 15.1 %copy-start.18 = (f32[1,1,256]{2,1,0:T(1,128)S(1)}, f32[1,1,256]{2,1,0:T(1,128)}, u32[]{:S(2)}) copy-start(f32[1,1,256]{2,1,0:T(1,128)} %get-tuple-element.61) | copy-start | bytes 3076
  221.3 24.3 %collective-permute-start.12 = (f32[1,256,1,256]{1,3,2,0:T(8,128)}, f32[1,256,1,256]{1,3,2,0:T(8,128)S(1)}, u32[]{:S(2)}, u32[]{:S(2)}) collective-permute-start(f32[1,256,1,256]{1,3,2,0:T(8,128)} %get-tuple-element.50), channel_id=1, source_target_pairs={{0,1},{1,2},{2,3},{3,4},{4,5},{5,6},{6,7},{8,9},{9,10},{10,11},{11... | collective-permute-start | bytes 786440 | tf_op jit(solution)/shard_map/ppermute | solution.py:15
  228.5 21.5 %collective-permute-start.13 = (f32[1,256,1,256]{1,3,2,0:T(8,128)}, f32[1,256,1,256]{1,3,2,0:T(8,128)S(1)}, u32[]{:S(2)}, u32[]{:S(2)}) collective-permute-start(f32[1,256,1,256]{1,3,2,0:T(8,128)} %get-tuple-element.51), channel_id=1, source_target_pairs={{1,0},{2,1},{3,2},{4,3},{5,4},{6,5},{7,6},{9,8},{10,9},{11,10},{12... | collective-permute-start | bytes 786440 | tf_op jit(solution)/shard_map/ppermute | solution.py:16
  237.2 394.4 %all-reduce.6.cloned.1.call-start = ((), (), s32[]{:S(2)}) async-start(), calls=%async_computation.1 | async-start | bytes 524288 | tf_op jit(solution)/shard_map/psum | solution.py:68
  251.9 108.2 %collective-permute-start.14 = (f32[1,256,10,1]{1,3,2,0:T(1,128)S(1)}, f32[1,256,10,1]{1,3,2,0:T(1,128)S(1)}, u32[]{:S(2)}, u32[]{:S(2)}) collective-permute-start(f32[1,256,10,1]{1,3,2,0:T(1,128)S(1)} %get-tuple-element.46), channel_id=1, source_target_pairs={{0,8},{8,16},{16,24},{24,32},{32,40},{40,48},{48,56},{56,64},{64,7... | collective-permute-start | bytes 30728 | tf_op jit(solution)/shard_map/ppermute | solution.py:15
  252.0 108.2 %collective-permute-start.15 = (f32[1,256,10,1]{1,3,2,0:T(1,128)S(1)}, f32[1,256,10,1]{1,3,2,0:T(1,128)S(1)}, u32[]{:S(2)}, u32[]{:S(2)}) collective-permute-start(f32[1,256,10,1]{1,3,2,0:T(1,128)S(1)} %get-tuple-element.47), channel_id=1, source_target_pairs={{8,0},{16,8},{24,16},{32,24},{40,32},{48,40},{56,48},{64,56},{72,6... | collective-permute-start | bytes 30728 | tf_op jit(solution)/shard_map/ppermute | solution.py:16
  370.3 300.0 %copy-start.25 = (s32[2]{0:T(128)S(1)}, s32[2]{0:T(128)}, u32[]{:S(2)}) copy-start(s32[2]{0:T(128)} %iota_multiply_fusion) | copy-start | bytes 28
  (20 other events, 107.0 us)
Sparse Core Ops, SparseCore 0:
  237.3 106.8 all-reduce.3
  360.2 271.3 all-reduce.5
